TPU v7x, 32 devices: a whole 2x2x4 slice. The times are simulated.
32 devices in a mesh: sample: 8 (over z, y), space: 4 (over x, core).
Axes of the slice: x: 2, y: 2, z: 4, core: 2. Of those that a mesh axis runs over, the one named last changes fastest.
Arguments:
- features: bfloat16 [8, 64, 256, 256], P('sample', 'space'), may hold values from -6 to 6
- weight_one: bfloat16 [3, 3, 256, 256], P(None, None, None, 'sample'), may hold values from -0.125 to 0.125
- offset_one: float32 [256], replicated, may hold values from -0.5 to 0.5
- weight_two: bfloat16 [3, 3, 256, 256], P(None, None, None, 'sample'), may hold values from -0.125 to 0.125
- offset_two: float32 [256], replicated, may hold values from -0.5 to 0.5
Outputs:
- context: bfloat16 [8, 64, 256, 256], P('sample', 'space')
All inputs are finite; a program needn't handle non-finite values.
Results may differ from a plain program's by a relative error of at most 0.0047.
Values may be sent and summed in bfloat16 or wider, within the bound.
A program may use at most 192 MiB of HBM per device.

v0:
```python
import jax
import jax.numpy as jnp
from jax import lax
from jax.sharding import PartitionSpec as P

DILATION_RATE = 8


def extended(block, sides, width):
    for axis, dim in sides:
        count = lax.axis_size(axis)
        forward = [(i, i + 1) for i in range(count - 1)]
        backward = [(target, source) for source, target in forward]
        low = lax.ppermute(
            lax.slice_in_dim(block, block.shape[dim] - width, None, axis=dim), axis, forward
        )
        high = lax.ppermute(lax.slice_in_dim(block, 0, width, axis=dim), axis, backward)
        block = jnp.concatenate([low, block, high], axis=dim)
    return block


def dilated(padded_input, kernel_weights, output_rows):
    tile_width = padded_input.shape[2]
    column_count = jnp.pad(padded_input, ((0, 0), (0, 0), (DILATION_RATE, DILATION_RATE), (0, 0)))
    tap_sum = None
    for row_offset_tap in range(3):
        for column_offset_tap in range(3):
            window = column_count[
                :,
                row_offset_tap * DILATION_RATE : row_offset_tap * DILATION_RATE + output_rows,
                column_offset_tap * DILATION_RATE : column_offset_tap * DILATION_RATE + tile_width,
                :,
            ]
            product = jnp.einsum(
                "shwc,co->shwo",
                window,
                kernel_weights[row_offset_tap, column_offset_tap],
                preferred_element_type=jnp.float32,
            )
            tap_sum = product if tap_sum is None else tap_sum + product
    return tap_sum


def first_layer(padded_input, weight_one, gathered, output_rows):
    gathered = lax.all_gather(weight_one, "sample", axis=3, tiled=True)
    return dilated(padded_input, gathered, output_rows)


def second_layer(padded_input, weight_two, gathered, output_rows):
    gathered = lax.all_gather(weight_two, "sample", axis=3, tiled=True)
    return dilated(padded_input, gathered, output_rows)


def with_rim(feature_values):
    return extended(feature_values, (("space", 1),), DILATION_RATE)


def per_device(features, weight_one, offset_one, weight_two, offset_two):
    rows_dev = features.shape[1]
    kernel_one, kernel_two = (None, None)
    tap_sum = first_layer(with_rim(features), weight_one, kernel_one, rows_dev)
    hidden = jnp.maximum(tap_sum + offset_one, 0.0).astype(jnp.bfloat16)
    hidden_rows = with_rim(hidden)
    result = second_layer(hidden_rows, weight_two, kernel_two, rows_dev)
    return jnp.maximum(result + offset_two, 0.0).astype(jnp.bfloat16)


def solution(mesh):
    return jax.shard_map(
        per_device,
        mesh=mesh,
        in_specs=(
            P("sample", "space", None, None),
            P(None, None, None, "sample"),
            P(),
            P(None, None, None, "sample"),
            P(),
        ),
        out_specs=P("sample", "space", None, None),
        check_vma=False,
    )
```

profile of v0, /device:TPU:1, one launch (start us, length us, event | category | flops | bytes accessed | tf_op | source)
XLA Modules:
  0.0 146.6 jit_solution(10417974059888261316)
XLA Ops:
  6.5 0.7 all-gather.3.cloned.1.call-update
  7.3 3.1 %fusion.43 = (bf16[1,8,256,256]{3,2,1,0:T(8,128)(2,1)}, bf16[1,8,256,256]{3,2,1,0:T(8,128)(2,1)}) fusion(bf16[1,16,256,256]{3,2,1,0:T(8,128)(2,1)} %param.5), kind=kLoop, calls=%fused_computation.79 | loop fusion | bytes 4194304 | tf_op jit(solution)/shard_map/slice | solution.py:15
  10.4 4.5 %collective-permute-start = (bf16[1,8,256,256]{3,2,1,0:T(8,128)(2,1)}, bf16[1,8,256,256]{3,2,1,0:T(8,128)(2,1)S(1)}, u32[]{:S(2)}, u32[]{:S(2)}) collective-permute-start(bf16[1,8,256,256]{3,2,1,0:T(8,128)(2,1)} %get-tuple-element.7), channel_id=1, source_target_pairs={{0,1},{1,2},{2,3},{4,5},{5,6},{6,7},{8,9},{9,10},{10,11},{12,13},{... | collective-permute-start | bytes 3145736 | tf_op jit(solution)/shard_map/ppermute | solution.py:14
  14.9 1.9 %collective-permute-start.1 = (bf16[1,8,256,256]{3,2,1,0:T(8,128)(2,1)}, bf16[1,8,256,256]{3,2,1,0:T(8,128)(2,1)}, u32[]{:S(2)}, u32[]{:S(2)}) collective-permute-start(bf16[1,8,256,256]{3,2,1,0:T(8,128)(2,1)} %get-tuple-element.8), channel_id=1, source_target_pairs={{1,0},{2,1},{3,2},{5,4},{6,5},{7,6},{9,8},{10,9},{11,10},{13,12},{... | collective-permute-start | bytes 3145736 | tf_op jit(solution)/shard_map/ppermute | solution.py:17
  16.8 10.1 %collective-permute-done = bf16[1,8,256,256]{3,2,1,0:T(8,128)(2,1)S(1)} collective-permute-done((bf16[1,8,256,256]{3,2,1,0:T(8,128)(2,1)}, bf16[1,8,256,256]{3,2,1,0:T(8,128)(2,1)S(1)}, u32[]{:S(2)}, u32[]{:S(2)}) %collective-permute-start) | collective-permute-done | bytes 1048608 | tf_op jit(solution)/shard_map/ppermute | solution.py:14
  26.9 4.7 %collective-permute-done.1 = bf16[1,8,256,256]{3,2,1,0:T(8,128)(2,1)} collective-permute-done((bf16[1,8,256,256]{3,2,1,0:T(8,128)(2,1)}, bf16[1,8,256,256]{3,2,1,0:T(8,128)(2,1)}, u32[]{:S(2)}, u32[]{:S(2)}) %collective-permute-start.1) | collective-permute-done | bytes 1048608 | tf_op jit(solution)/shard_map/ppermute | solution.py:17
  31.6 3.5 %fusion.5 = bf16[1,32,272,256]{3,2,1,0:T(8,128)(2,1)} fusion(bf16[1,8,256,256]{3,2,1,0:T(8,128)(2,1)} %collective-permute-done.1, bf16[1,16,256,256]{3,2,1,0:T(8,128)(2,1)S(1)} %copy-done.1, bf16[1,8,256,256]{3,2,1,0:T(8,128)(2,1)S(1)} %collective-permute-done), kind=kLoop, calls=%fused_computation.9 | loop fusion | flops 26738688 | bytes 8650752 | tf_op jit(solution)/shard_map/concatenate | solution.py:18
  35.1 16.4 %all-gather.3.cloned.1.call-done = bf16[3,3,256,256]{2,3,1,0:T(8,128)(2,1)} async-done(((bf16[3,3,256,32]{2,3,1,0:T(8,128)(2,1)}), bf16[3,3,256,256]{2,3,1,0:T(8,128)(2,1)}) %all-gather.3.cloned.1.call-update) | async-done | bytes 1179664 | tf_op jit(solution)/shard_map/all_gather | solution.py:45
  51.5 4.5 %fusion.25 = f32[16,256,256]{2,1,0:T(8,128)} fusion(bf16[1,32,272,256]{3,2,1,0:T(8,128)(2,1)} %fusion.5, bf16[3,3,256,256]{2,3,1,0:T(8,128)(2,1)} %all-gather.3.cloned.1.call-done), kind=kOutput, calls=%fused_computation.39 | convolution fusion | flops 536870912 | bytes 6422528 | tf_op jit(solution)/shard_map/shwc,co->shwo/dot_general | solution.py:34
  56.1 2.7 %fusion.26 = f32[16,256,256]{2,1,0:T(8,128)} fusion(bf16[1,32,272,256]{3,2,1,0:T(8,128)(2,1)S(1)} %copy-done, bf16[3,3,256,256]{2,3,1,0:T(8,128)(2,1)S(1)} %copy-done.6), kind=kOutput, calls=%fused_computation.41 | convolution fusion | flops 536870912 | bytes 6422528 | tf_op jit(solution)/shard_map/shwc,co->shwo/dot_general | solution.py:34
  58.8 2.7 %fusion.27 = f32[16,256,256]{2,1,0:T(8,128)} fusion(bf16[1,32,272,256]{3,2,1,0:T(8,128)(2,1)S(1)} %copy-done, bf16[3,3,256,256]{2,3,1,0:T(8,128)(2,1)S(1)} %copy-done.6), kind=kOutput, calls=%fused_computation.43 | convolution fusion | flops 536870912 | bytes 6422528 | tf_op jit(solution)/shard_map/shwc,co->shwo/dot_general | solution.py:34
  61.5 2.7 %fusion.28 = f32[16,256,256]{2,1,0:T(8,128)} fusion(bf16[1,32,272,256]{3,2,1,0:T(8,128)(2,1)S(1)} %copy-done, bf16[3,3,256,256]{2,3,1,0:T(8,128)(2,1)S(1)} %copy-done.6), kind=kOutput, calls=%fused_computation.45 | convolution fusion | flops 536870912 | bytes 6422528 | tf_op jit(solution)/shard_map/shwc,co->shwo/dot_general | solution.py:34
  64.2 2.7 %fusion.33 = f32[16,256,256]{2,1,0:T(8,128)} fusion(bf16[1,32,272,256]{3,2,1,0:T(8,128)(2,1)S(1)} %copy-done, bf16[3,3,256,256]{2,3,1,0:T(8,128)(2,1)S(1)} %copy-done.6), kind=kOutput, calls=%fused_computation.51 | convolution fusion | flops 536870912 | bytes 6422528 | tf_op jit(solution)/shard_map/shwc,co->shwo/dot_general | solution.py:34
  66.9 2.1 %fusion.22 = f32[16,256,256]{2,1,0:T(8,128)S(1)} fusion(bf16[1,8,256,256]{3,2,1,0:T(8,128)(2,1)} %collective-permute-done.1, bf16[1,16,256,256]{3,2,1,0:T(8,128)(2,1)S(1)} %copy-done.1, bf16[3,3,256,256]{2,3,1,0:T(8,128)(2,1)S(1)} %copy-done.6), kind=kOutput, calls=%fused_computation.36 | convolution fusion | flops 537919488 | bytes 7471104 | tf_op jit(solution)/shard_map/shwc,co->shwo/dot_general | solution.py:34
  68.9 2.7 %fusion.30 = f32[16,256,256]{2,1,0:T(8,128)} fusion(bf16[1,16,256,256]{3,2,1,0:T(8,128)(2,1)S(1)} %copy-done.1, bf16[1,8,256,256]{3,2,1,0:T(8,128)(2,1)S(1)} %copy-done.3, bf16[3,3,256,256]{2,3,1,0:T(8,128)(2,1)S(1)} %copy-done.6), kind=kOutput, calls=%fused_computation.48 | convolution fusion | flops 537919488 | bytes 7471104 | tf_op jit(solution)/shard_map/shwc,co->shwo/dot_general | solution.py:34
  71.7 2.8 %fusion.34 = f32[16,256,256]{2,1,0:T(8,128)} fusion(bf16[1,16,256,256]{3,2,1,0:T(8,128)(2,1)S(1)} %copy-done.1, bf16[3,3,256,256]{2,3,1,0:T(8,128)(2,1)S(1)} %copy-done.6), kind=kOutput, calls=%fused_computation.52 | convolution fusion | flops 536870912 | bytes 6422528 | tf_op jit(solution)/shard_map/shwc,co->shwo/dot_general | solution.py:34
  74.5 10.8 %maximum_convert_fusion.1 = bf16[16,256,256]{2,1,0:T(8,128)(2,1)S(1)} fusion(f32[16,256,256]{2,1,0:T(8,128)S(1)} %fusion.22, f32[16,256,256]{2,1,0:T(8,128)} %fusion.25, f32[16,256,256]{2,1,0:T(8,128)} %fusion.26, f32[16,256,256]{2,1,0:T(8,128)} %fusion.34, f32[16,256,256]{2,1,0:T(8,128)} %fusion.27, f32[16,256,256]{2,1,0:T(8,128)} %fusion.28, ...), kind=kOutput, calls=%fused_computation.11 | convolution fusion | flops 548405248 | bytes 37880832 | tf_op jit(solution)/shard_map/shwc,co->shwo/dot_general | solution.py:34
  85.3 1.5 %fusion.42 = (bf16[1,8,256,256]{3,2,1,0:T(8,128)(2,1)}, bf16[1,8,256,256]{3,2,1,0:T(8,128)(2,1)}) fusion(bf16[1,16,256,256]{3,2,1,0:T(8,128)(2,1)S(1)} %bitcast.169), kind=kLoop, calls=%fused_computation.78 | loop fusion | bytes 4194304 | tf_op jit(solution)/shard_map/slice | solution.py:15
  86.8 4.9 %collective-permute-start.2 = (bf16[1,8,256,256]{3,2,1,0:T(8,128)(2,1)}, bf16[1,8,256,256]{3,2,1,0:T(8,128)(2,1)S(1)}, u32[]{:S(2)}, u32[]{:S(2)}) collective-permute-start(bf16[1,8,256,256]{3,2,1,0:T(8,128)(2,1)} %get-tuple-element.5), channel_id=1, source_target_pairs={{0,1},{1,2},{2,3},{4,5},{5,6},{6,7},{8,9},{9,10},{10,11},{12,13},{... | collective-permute-start | bytes 3145736 | tf_op jit(solution)/shard_map/ppermute | solution.py:14
  91.7 2.1 %collective-permute-start.3 = (bf16[1,8,256,256]{3,2,1,0:T(8,128)(2,1)}, bf16[1,8,256,256]{3,2,1,0:T(8,128)(2,1)}, u32[]{:S(2)}, u32[]{:S(2)}) collective-permute-start(bf16[1,8,256,256]{3,2,1,0:T(8,128)(2,1)} %get-tuple-element.6), channel_id=1, source_target_pairs={{1,0},{2,1},{3,2},{5,4},{6,5},{7,6},{9,8},{10,9},{11,10},{13,12},{... | collective-permute-start | bytes 3145736 | tf_op jit(solution)/shard_map/ppermute | solution.py:17
  93.8 3.7 %fusion.37 = f32[16,256,256]{2,1,0:T(8,128)} fusion(bf16[16,256,256]{2,1,0:T(8,128)(2,1)S(1)} %maximum_convert_fusion.1, bf16[3,3,256,256]{2,3,1,0:T(8,128)(2,1)} %all-gather.5.cloned.1.call-done), kind=kOutput, calls=%fused_computation.60 | convolution fusion | flops 536870912 | bytes 6422528 | tf_op jit(solution)/shard_map/shwc,co->shwo/dot_general | solution.py:34
  97.5 6.2 %collective-permute-done.2 = bf16[1,8,256,256]{3,2,1,0:T(8,128)(2,1)S(1)} collective-permute-done((bf16[1,8,256,256]{3,2,1,0:T(8,128)(2,1)}, bf16[1,8,256,256]{3,2,1,0:T(8,128)(2,1)S(1)}, u32[]{:S(2)}, u32[]{:S(2)}) %collective-permute-start.2) | collective-permute-done | bytes 1048608 | tf_op jit(solution)/shard_map/ppermute | solution.py:14
  103.7 0.7 fusion.16
  104.7 3.4 %collective-permute-done.3 = bf16[1,8,256,256]{3,2,1,0:T(8,128)(2,1)} collective-permute-done((bf16[1,8,256,256]{3,2,1,0:T(8,128)(2,1)}, bf16[1,8,256,256]{3,2,1,0:T(8,128)(2,1)}, u32[]{:S(2)}, u32[]{:S(2)}) %collective-permute-start.3) | collective-permute-done | bytes 1048608 | tf_op jit(solution)/shard_map/ppermute | solution.py:17
  108.1 2.1 %select_maximum_fusion = bf16[1,32,272,256]{3,2,1,0:T(8,128)(2,1)S(1)} fusion(bf16[1,8,256,256]{3,2,1,0:T(8,128)(2,1)} %collective-permute-done.3, bf16[1,16,256,256]{3,2,1,0:T(8,128)(2,1)S(1)} %bitcast.171, bf16[1,8,256,256]{3,2,1,0:T(8,128)(2,1)} %copy-done.4), kind=kLoop, calls=%fused_computation.3 | loop fusion | flops 26738688 | bytes 8650752 | tf_op jit(solution)/shard_map/concatenate | solution.py:18
  110.2 2.7 %fusion.11 = f32[16,256,256]{2,1,0:T(8,128)} fusion(bf16[1,32,272,256]{3,2,1,0:T(8,128)(2,1)S(1)} %select_maximum_fusion, bf16[3,3,256,256]{2,3,1,0:T(8,128)(2,1)S(1)} %copy-done.5), kind=kOutput, calls=%fused_computation.19 | convolution fusion | flops 536870912 | bytes 6422528 | tf_op jit(solution)/shard_map/shwc,co->shwo/dot_general | solution.py:34
  112.9 2.7 %fusion.12 = f32[16,256,256]{2,1,0:T(8,128)} fusion(bf16[1,32,272,256]{3,2,1,0:T(8,128)(2,1)S(1)} %select_maximum_fusion, bf16[3,3,256,256]{2,3,1,0:T(8,128)(2,1)S(1)} %copy-done.5), kind=kOutput, calls=%fused_computation.21 | convolution fusion | flops 536870912 | bytes 6422528 | tf_op jit(solution)/shard_map/shwc,co->shwo/dot_general | solution.py:34
  115.6 2.7 %fusion.13 = f32[16,256,256]{2,1,0:T(8,128)} fusion(bf16[1,32,272,256]{3,2,1,0:T(8,128)(2,1)S(1)} %select_maximum_fusion, bf16[3,3,256,256]{2,3,1,0:T(8,128)(2,1)S(1)} %copy-done.5), kind=kOutput, calls=%fused_computation.23 | convolution fusion | flops 536870912 | bytes 6422528 | tf_op jit(solution)/shard_map/shwc,co->shwo/dot_general | solution.py:34
  118.3 2.7 %fusion.14 = f32[16,256,256]{2,1,0:T(8,128)} fusion(bf16[1,32,272,256]{3,2,1,0:T(8,128)(2,1)S(1)} %select_maximum_fusion, bf16[3,3,256,256]{2,3,1,0:T(8,128)(2,1)S(1)} %copy-done.5), kind=kOutput, calls=%fused_computation.25 | convolution fusion | flops 536870912 | bytes 6422528 | tf_op jit(solution)/shard_map/shwc,co->shwo/dot_general | solution.py:34
  121.0 2.7 %fusion.19 = f32[16,256,256]{2,1,0:T(8,128)} fusion(bf16[1,32,272,256]{3,2,1,0:T(8,128)(2,1)S(1)} %select_maximum_fusion, bf16[3,3,256,256]{2,3,1,0:T(8,128)(2,1)S(1)} %copy-done.5), kind=kOutput, calls=%fused_computation.31 | convolution fusion | flops 536870912 | bytes 6422528 | tf_op jit(solution)/shard_map/shwc,co->shwo/dot_general | solution.py:34
  123.7 4.0 %fusion.8 = f32[16,256,256]{2,1,0:T(8,128)} fusion(bf16[1,8,256,256]{3,2,1,0:T(8,128)(2,1)} %collective-permute-done.3, bf16[1,16,256,256]{3,2,1,0:T(8,128)(2,1)S(1)} %bitcast.172, bf16[3,3,256,256]{2,3,1,0:T(8,128)(2,1)S(1)} %copy-done.5), kind=kOutput, calls=%fused_computation.16 | convolution fusion | flops 537919488 | bytes 7471104 | tf_op jit(solution)/shard_map/shwc,co->shwo/dot_general | solution.py:34
  127.7 12.1 %fusion.36 = bf16[1,16,256,256]{3,2,1,0:T(8,128)(2,1)} fusion(f32[256]{0:T(256)S(1)} %copy-done.8, bf16[1,32,272,256]{3,2,1,0:T(8,128)(2,1)S(1)} %select_maximum_fusion, f32[16,256,256]{2,1,0:T(8,128)} %fusion.8, f32[16,256,256]{2,1,0:T(8,128)} %fusion.11, f32[16,256,256]{2,1,0:T(8,128)} %fusion.12, f32[16,256,256]{2,1,0:T(8,128)} %fusion.37, ...), kind=kOutput, calls=%fused_computation.54 | convolution fusion | flops 548405248 | bytes 37880832 | tf_op jit(solution)/shard_map/shwc,co->shwo/dot_general | solution.py:34
  (22 shorter events, 0.3 us)
Async XLA Ops:
  6.5 25.1 %copy-start.1 = (bf16[1,16,256,256]{3,2,1,0:T(8,128)(2,1)S(1)}, bf16[1,16,256,256]{3,2,1,0:T(8,128)(2,1)}, u32[]{:S(2)}) copy-start(bf16[1,16,256,256]{3,2,1,0:T(8,128)(2,1)} %param.5) | copy-start | bytes 6291460
  6.5 45.0 %all-gather.3.cloned.1.call-start = ((), (), s32[]{:S(2)}) async-start(), calls=%async_computation | async-start | bytes 1327104 | tf_op jit(solution)/shard_map/all_gather | solution.py:45
  7.3 86.6 %all-gather.5.cloned.1.call-start = ((), (), s32[]{:S(2)}) async-start(), calls=%async_computation.1 | async-start | bytes 1327104 | tf_op jit(solution)/shard_map/all_gather | solution.py:50
  10.4 16.5 %collective-permute-start = (bf16[1,8,256,256]{3,2,1,0:T(8,128)(2,1)}, bf16[1,8,256,256]{3,2,1,0:T(8,128)(2,1)S(1)}, u32[]{:S(2)}, u32[]{:S(2)}) collective-permute-start(bf16[1,8,256,256]{3,2,1,0:T(8,128)(2,1)} %get-tuple-element.7), channel_id=1, source_target_pairs={{0,1},{1,2},{2,3},{4,5},{5,6},{6,7},{8,9},{9,10},{10,11},{12,13},{... | collective-permute-start | bytes 3145736 | tf_op jit(solution)/shard_map/ppermute | solution.py:14
  14.9 16.7 %collective-permute-start.1 = (bf16[1,8,256,256]{3,2,1,0:T(8,128)(2,1)}, bf16[1,8,256,256]{3,2,1,0:T(8,128)(2,1)}, u32[]{:S(2)}, u32[]{:S(2)}) collective-permute-start(bf16[1,8,256,256]{3,2,1,0:T(8,128)(2,1)} %get-tuple-element.8), channel_id=1, source_target_pairs={{1,0},{2,1},{3,2},{5,4},{6,5},{7,6},{9,8},{10,9},{11,10},{13,12},{... | collective-permute-start | bytes 3145736 | tf_op jit(solution)/shard_map/ppermute | solution.py:17
  26.9 8.2 %copy-start.2 = (bf16[1,8,256,256]{3,2,1,0:T(8,128)(2,1)}, bf16[1,8,256,256]{3,2,1,0:T(8,128)(2,1)S(1)}, u32[]{:S(2)}) copy-start(bf16[1,8,256,256]{3,2,1,0:T(8,128)(2,1)S(1)} %collective-permute-done) | copy-start | bytes 3145732
  51.5 4.5 %copy-start = (bf16[1,32,272,256]{3,2,1,0:T(8,128)(2,1)S(1)}, bf16[1,32,272,256]{3,2,1,0:T(8,128)(2,1)}, u32[]{:S(2)}) copy-start(bf16[1,32,272,256]{3,2,1,0:T(8,128)(2,1)} %fusion.5) | copy-start | bytes 13369348
  51.5 4.5 %copy-start.6 = (bf16[3,3,256,256]{2,3,1,0:T(8,128)(2,1)S(1)}, bf16[3,3,256,256]{2,3,1,0:T(8,128)(2,1)}, u32[]{:S(2)}) copy-start(bf16[3,3,256,256]{2,3,1,0:T(8,128)(2,1)} %all-gather.3.cloned.1.call-done) | copy-start | bytes 3538948
  66.9 2.1 %copy-start.3 = (bf16[1,8,256,256]{3,2,1,0:T(8,128)(2,1)S(1)}, bf16[1,8,256,256]{3,2,1,0:T(8,128)(2,1)}, u32[]{:S(2)}) copy-start(bf16[1,8,256,256]{3,2,1,0:T(8,128)(2,1)} %copy-done.2) | copy-start | bytes 3145732
  71.7 2.8 %copy-start.7 = (f32[256]{0:T(256)S(1)}, f32[256]{0:T(256)}, u32[]{:S(2)}) copy-start(f32[256]{0:T(256)} %param.7) | copy-start | bytes 3076
  86.8 16.9 %collective-permute-start.2 = (bf16[1,8,256,256]{3,2,1,0:T(8,128)(2,1)}, bf16[1,8,256,256]{3,2,1,0:T(8,128)(2,1)S(1)}, u32[]{:S(2)}, u32[]{:S(2)}) collective-permute-start(bf16[1,8,256,256]{3,2,1,0:T(8,128)(2,1)} %get-tuple-element.5), channel_id=1, source_target_pairs={{0,1},{1,2},{2,3},{4,5},{5,6},{6,7},{8,9},{9,10},{10,11},{12,13},{... | collective-permute-start | bytes 3145736 | tf_op jit(solution)/shard_map/ppermute | solution.py:14
  91.7 16.4 %collective-permute-start.3 = (bf16[1,8,256,256]{3,2,1,0:T(8,128)(2,1)}, bf16[1,8,256,256]{3,2,1,0:T(8,128)(2,1)}, u32[]{:S(2)}, u32[]{:S(2)}) collective-permute-start(bf16[1,8,256,256]{3,2,1,0:T(8,128)(2,1)} %get-tuple-element.6), channel_id=1, source_target_pairs={{1,0},{2,1},{3,2},{5,4},{6,5},{7,6},{9,8},{10,9},{11,10},{13,12},{... | collective-permute-start | bytes 3145736 | tf_op jit(solution)/shard_map/ppermute | solution.py:17
  93.8 9.9 %copy-start.5 = (bf16[3,3,256,256]{2,3,1,0:T(8,128)(2,1)S(1)}, bf16[3,3,256,256]{2,3,1,0:T(8,128)(2,1)}, u32[]{:S(2)}) copy-start(bf16[3,3,256,256]{2,3,1,0:T(8,128)(2,1)} %all-gather.5.cloned.1.call-done) | copy-start | bytes 3538948
  103.7 1.0 copy-start.4
  123.7 4.0 %copy-start.8 = (f32[256]{0:T(256)S(1)}, f32[256]{0:T(256)}, u32[]{:S(2)}) copy-start(f32[256]{0:T(256)} %param.9) | copy-start | bytes 3076
Sparse Core Ops, SparseCore 0:
  9.5 41.9 all-gather.2
  53.7 39.8 all-gather.4
where the time goes:
time: 147 us
  matrix products  67.7 us (46%)
  waiting for transfers between devices  41.6 us (28%)
  starting transfers between devices  13.5 us (9%)
  between operations  13.5 us (9%)
  other arithmetic  5.53 us (4%)
  local copies, waits for them, and re-layouts  4.85 us (3%)
    dot_general x18, matrix products, dilated(): jnp.einsum('shwc,co->shwo', window, kernel_weights[row_offset_tap, column...  67.7 us
    all_gather x1, waiting for transfers between devices, first_layer(): gathered = lax.all_gather(weight_one, 'sample', axis=3, tiled=True)  16.4 us
    ppermute x2, waiting for transfers between devices, extended(): lax.ppermute(lax.slice_in_dim(block, block.shape[dim] - width, None, axis...  16.3 us
    ppermute x2, starting transfers between devices, extended(): lax.ppermute(lax.slice_in_dim(block, block.shape[dim] - width, None, axis...  9.39 us
    ppermute x2, waiting for transfers between devices, extended(): lax.ppermute(lax.slice_in_dim(block, 0, width, axis=dim), axis, backward)  8.11 us
    concatenate x2, other arithmetic, extended(): block = jnp.concatenate([low, block, high], axis=dim)  5.53 us
    slice x2, local copies, waits for them, and re-layouts, extended(): lax.slice_in_dim(block, block.shape[dim] - width, None, axis=dim)  4.59 us
    ppermute x2, starting transfers between devices, extended(): lax.ppermute(lax.slice_in_dim(block, 0, width, axis=dim), axis, backward)  4.02 us
  transfers between devices with their start and end apart: 6, of which 5 were waited for; matrix products, arithmetic and copies ran while one was open for 31% of the time, Pallas kernels for 0%

commit v1 on v0

--- a/solution.py
+++ b/solution.py
@@ -42,7 +42,15 @@
 
 
 def first_layer(padded_input, weight_one, gathered, output_rows):
-    gathered = lax.all_gather(weight_one, "sample", axis=3, tiled=True)
+    ways, here, step = (lax.axis_size("sample"), lax.axis_index("sample"), weight_one.shape[3])
+    line, have = (weight_one, 1)
+    while have < ways:
+        line = jnp.concatenate(
+            [line, lax.ppermute(line, "sample", [(d, (d - have) % ways) for d in range(ways)])],
+            axis=3,
+        )
+        have = 2 * have
+    gathered = jnp.roll(line, here * step, axis=3)
     return dilated(padded_input, gathered, output_rows)
 
 

time: 147 us -> 172 us (1.17)
  local copies, waits for them, and re-layouts: 4.85 us -> 13.8 us
  matrix products: 67.7 us -> 74.6 us
  starting transfers between devices: 13.5 us -> 19.4 us
  waiting for transfers between devices: 41.6 us -> 43.7 us
    ppermute x0 -> x3, waiting for transfers between devices: none -> 35.7 us  [first_layer(): lax.ppermute(line, 'sample', [(d, (d - have) % ways) for d in range(ways)])]
    all_gather x1 -> x0, waiting for transfers between devices: 16.4 us -> none  [first_layer(): gathered = lax.all_gather(weight_one, 'sample', axis=3, tiled=True)]
    ppermute x2, waiting for transfers between devices: 16.3 us -> 6.19 us  [extended(): lax.ppermute(lax.slice_in_dim(block, block.shape[dim] - width, None, axis...]
    dot_general x18, matrix products: 67.7 us -> 74.6 us  [dilated(): jnp.einsum('shwc,co->shwo', window, kernel_weights[row_offset_tap, column...]
    concatenate x0 -> x1, local copies, waits for them, and re-layouts: none -> 6.83 us  [first_layer(): gathered = jnp.roll(line, here * step, axis=3)]
    ppermute x2, waiting for transfers between devices: 8.11 us -> 1.71 us  [extended(): lax.ppermute(lax.slice_in_dim(block, 0, width, axis=dim), axis, backward)]
    ppermute x0 -> x3, starting transfers between devices: none -> 6.3 us  [first_layer(): lax.ppermute(line, 'sample', [(d, (d - have) % ways) for d in range(ways)])]
    concatenate x0 -> x2, other arithmetic: none -> 2.29 us  [first_layer(): jnp.concatenate([line, lax.ppermute(line, 'sample', [(d, (d - have) % way...]
  transfers between devices with their start and end apart: 6 -> 8, of which waited for: 5 -> 4; matrix products, arithmetic and copies ran while one was open for 31% -> 35% of each run, Pallas kernels for 0% -> 0%
where the time goes in v1:
time: 172 us; the launch traced here: 171 us
  matrix products  74.6 us (43%)
  waiting for transfers between devices  43.7 us (25%)
  starting transfers between devices  19.4 us (11%)
  local copies, waits for them, and re-layouts  13.8 us (8%)
  between operations  13.6 us (8%)
  other arithmetic  6.28 us (4%)
    dot_general x18, matrix products, dilated(): jnp.einsum('shwc,co->shwo', window, kernel_weights[row_offset_tap, column...  74.6 us
    ppermute x3, waiting for transfers between devices, first_layer(): lax.ppermute(line, 'sample', [(d, (d - have) % ways) for d in range(ways)])  35.7 us
    ppermute x2, starting transfers between devices, extended(): lax.ppermute(lax.slice_in_dim(block, block.shape[dim] - width, None, axis...  9.07 us
    concatenate x1, local copies, waits for them, and re-layouts, first_layer(): gathered = jnp.roll(line, here * step, axis=3)  6.83 us
    ppermute x3, starting transfers between devices, first_layer(): lax.ppermute(line, 'sample', [(d, (d - have) % ways) for d in range(ways)])  6.3 us
    ppermute x2, waiting for transfers between devices, extended(): lax.ppermute(lax.slice_in_dim(block, block.shape[dim] - width, None, axis...  6.19 us
    slice x2, local copies, waits for them, and re-layouts, extended(): lax.slice_in_dim(block, block.shape[dim] - width, None, axis=dim)  4.51 us
    ppermute x2, starting transfers between devices, extended(): lax.ppermute(lax.slice_in_dim(block, 0, width, axis=dim), axis, backward)  4.02 us
  transfers between devices with their start and end apart: 8, of which 4 were waited for; matrix products, arithmetic and copies ran while one was open for 35% of the time, Pallas kernels for 0%

profile of v1, /device:TPU:1, one launch (start us, length us, event | category | flops | bytes accessed | tf_op | source)
XLA Modules:
  0.0 171.3 jit_solution(10337348875329322921)
XLA Ops:
  6.5 5.1 %collective-permute-start.2 = (bf16[3,3,256,32]{2,3,1,0:T(8,128)(2,1)}, bf16[3,3,256,32]{2,3,1,0:T(8,128)(2,1)S(1)}, u32[]{:S(2)}, u32[]{:S(2)}) collective-permute-start(bf16[3,3,256,32]{2,3,1,0:T(8,128)(2,1)} %param.6), channel_id=1, source_target_pairs={{0,28},{4,0},{8,4},{12,8},{16,12},{20,16},{24,20},{28,24},{1,29},{... | collective-permute-start | bytes 442376 | tf_op jit(solution)/shard_map/ppermute | solution.py:49
  11.6 2.8 %collective-permute-done.2 = bf16[3,3,256,32]{2,3,1,0:T(8,128)(2,1)S(1)} collective-permute-done((bf16[3,3,256,32]{2,3,1,0:T(8,128)(2,1)}, bf16[3,3,256,32]{2,3,1,0:T(8,128)(2,1)S(1)}, u32[]{:S(2)}, u32[]{:S(2)}) %collective-permute-start.2) | collective-permute-done | bytes 147488 | tf_op jit(solution)/shard_map/ppermute | solution.py:49
  16.6 3.1 %fusion.59 = (bf16[1,8,256,256]{3,2,1,0:T(8,128)(2,1)}, bf16[1,8,256,256]{3,2,1,0:T(8,128)(2,1)}) fusion(bf16[1,16,256,256]{3,2,1,0:T(8,128)(2,1)} %param.5), kind=kLoop, calls=%fused_computation.97 | loop fusion | bytes 4194304 | tf_op jit(solution)/shard_map/slice | solution.py:15
  19.7 4.8 %collective-permute-start = (bf16[1,8,256,256]{3,2,1,0:T(8,128)(2,1)}, bf16[1,8,256,256]{3,2,1,0:T(8,128)(2,1)}, u32[]{:S(2)}, u32[]{:S(2)}) collective-permute-start(bf16[1,8,256,256]{3,2,1,0:T(8,128)(2,1)} %get-tuple-element.7), channel_id=1, source_target_pairs={{0,1},{1,2},{2,3},{4,5},{5,6},{6,7},{8,9},{9,10},{10,11},{12,13},{... | collective-permute-start | bytes 3145736 | tf_op jit(solution)/shard_map/ppermute | solution.py:14
  24.5 1.9 %collective-permute-start.1 = (bf16[1,8,256,256]{3,2,1,0:T(8,128)(2,1)}, bf16[1,8,256,256]{3,2,1,0:T(8,128)(2,1)}, u32[]{:S(2)}, u32[]{:S(2)}) collective-permute-start(bf16[1,8,256,256]{3,2,1,0:T(8,128)(2,1)} %get-tuple-element.8), channel_id=1, source_target_pairs={{1,0},{2,1},{3,2},{5,4},{6,5},{7,6},{9,8},{10,9},{11,10},{13,12},{... | collective-permute-start | bytes 3145736 | tf_op jit(solution)/shard_map/ppermute | solution.py:17
  29.7 32.9 %collective-permute-done.4 = bf16[3,3,256,128]{3,2,1,0:T(8,128)(2,1)} collective-permute-done((bf16[3,3,256,128]{3,2,1,0:T(8,128)(2,1)}, bf16[3,3,256,128]{3,2,1,0:T(8,128)(2,1)}, u32[]{:S(2)}, u32[]{:S(2)}) %collective-permute-start.4) | collective-permute-done | bytes 589856 | tf_op jit(solution)/shard_map/ppermute | solution.py:49
  62.6 6.8 %concatenate.35 = bf16[3,3,256,512]{3,2,1,0:T(8,128)(2,1)} concatenate(bf16[3,3,256,32]{3,2,1,0:T(8,128)(2,1)S(1)} %copy.15, bf16[3,3,256,32]{3,2,1,0:T(8,128)(2,1)S(1)} %copy.16, bf16[3,3,256,64]{3,2,1,0:T(8,128)(2,1)} %copy-done.2, bf16[3,3,256,128]{3,2,1,0:T(8,128)(2,1)} %collective-permute-done.4, bf16[3,3,256,32]{3,2,1,0:T(8,128)(2,1)S(1)} %copy.15, ...), dimensions={3} | concatenate | bytes 4718592 | tf_op jit(solution)/shard_map/jit(_roll_dynamic)/concatenate | solution.py:53
  69.4 1.7 fusion.41
  71.1 2.0 %fusion.5 = bf16[1,32,272,256]{3,2,1,0:T(8,128)(2,1)S(1)} fusion(bf16[1,8,256,256]{3,2,1,0:T(8,128)(2,1)} %collective-permute-done.1, bf16[1,16,256,256]{3,2,1,0:T(8,128)(2,1)S(1)} %copy-done, bf16[1,8,256,256]{3,2,1,0:T(8,128)(2,1)} %collective-permute-done), kind=kLoop, calls=%fused_computation.9 | loop fusion | flops 26738688 | bytes 8650752 | tf_op jit(solution)/shard_map/concatenate | solution.py:18
  73.2 3.7 %fusion.34 = f32[16,256,256]{2,1,0:T(8,128)} fusion(bf16[1,32,272,256]{3,2,1,0:T(8,128)(2,1)S(1)} %fusion.5, bf16[3,3,256,512]{3,2,1,0:T(8,128)(2,1)} %concatenate.35, s32[]{:T(128)S(6)} %add.118, s32[]{:T(128)S(6)} %select_n.14), kind=kOutput, calls=%fused_computation.50 | convolution fusion | flops 536870912 | bytes 6422536 | tf_op jit(solution)/shard_map/shwc,co->shwo/dot_general | solution.py:34
  76.8 3.7 %fusion.33 = f32[16,256,256]{2,1,0:T(8,128)} fusion(bf16[1,32,272,256]{3,2,1,0:T(8,128)(2,1)S(1)} %fusion.5, bf16[3,3,256,512]{3,2,1,0:T(8,128)(2,1)} %concatenate.35, s32[]{:T(128)S(6)} %add.118, s32[]{:T(128)S(6)} %add.119, s32[]{:T(128)S(6)} %select_n.14), kind=kOutput, calls=%fused_computation.48 | convolution fusion | flops 536870912 | bytes 6422540 | tf_op jit(solution)/shard_map/shwc,co->shwo/dot_general | solution.py:34
  80.5 3.6 %fusion.35 = f32[16,256,256]{2,1,0:T(8,128)} fusion(bf16[1,32,272,256]{3,2,1,0:T(8,128)(2,1)S(1)} %fusion.5, bf16[3,3,256,512]{3,2,1,0:T(8,128)(2,1)} %concatenate.35, s32[]{:T(128)S(6)} %add.119, s32[]{:T(128)S(6)} %select_n.14), kind=kOutput, calls=%fused_computation.52 | convolution fusion | flops 536870912 | bytes 6422536 | tf_op jit(solution)/shard_map/shwc,co->shwo/dot_general | solution.py:34
  84.1 3.6 %fusion.40 = f32[16,256,256]{2,1,0:T(8,128)} fusion(bf16[1,32,272,256]{3,2,1,0:T(8,128)(2,1)S(1)} %fusion.5, bf16[3,3,256,512]{3,2,1,0:T(8,128)(2,1)} %concatenate.35, s32[]{:T(128)S(6)} %select_n.14), kind=kOutput, calls=%fused_computation.58 | convolution fusion | flops 536870912 | bytes 6422532 | tf_op jit(solution)/shard_map/shwc,co->shwo/dot_general | solution.py:34
  87.7 3.6 %fusion.32 = f32[16,256,256]{2,1,0:T(8,128)} fusion(bf16[1,32,272,256]{3,2,1,0:T(8,128)(2,1)S(1)} %fusion.5, bf16[3,3,256,512]{3,2,1,0:T(8,128)(2,1)} %concatenate.35, s32[]{:T(128)S(6)} %add.119, s32[]{:T(128)S(6)} %select_n.14), kind=kOutput, calls=%fused_computation.46 | convolution fusion | flops 536870912 | bytes 6422536 | tf_op jit(solution)/shard_map/shwc,co->shwo/dot_general | solution.py:34
  91.4 4.0 %fusion.37 = f32[16,256,256]{2,1,0:T(8,128)} fusion(bf16[1,16,256,256]{3,2,1,0:T(8,128)(2,1)S(1)} %copy-done, bf16[1,8,256,256]{3,2,1,0:T(8,128)(2,1)} %collective-permute-done, bf16[3,3,256,512]{3,2,1,0:T(8,128)(2,1)} %concatenate.35, s32[]{:T(128)S(6)} %add.118, s32[]{:T(128)S(6)} %select_n.14), kind=kOutput, calls=%fused_computation.55 | convolution fusion | flops 537919488 | bytes 7471112 | tf_op jit(solution)/shard_map/shwc,co->shwo/dot_general | solution.py:34
  95.4 4.0 %fusion.29 = f32[16,256,256]{2,1,0:T(8,128)} fusion(bf16[1,8,256,256]{3,2,1,0:T(8,128)(2,1)} %collective-permute-done.1, bf16[1,16,256,256]{3,2,1,0:T(8,128)(2,1)S(1)} %copy-done, bf16[3,3,256,512]{3,2,1,0:T(8,128)(2,1)} %concatenate.35, s32[]{:T(128)S(6)} %add.119, s32[]{:T(128)S(6)} %add.118, s32[]{:T(128)S(6)} %select_n.14), kind=kOutput, calls=%fused_computation.43 | convolution fusion | flops 537919488 | bytes 7471116 | tf_op jit(solution)/shard_map/shwc,co->shwo/dot_general | solution.py:34
  99.4 10.6 %fusion.12 = bf16[16,256,256]{2,1,0:T(8,128)(2,1)S(1)} fusion(f32[16,256,256]{2,1,0:T(8,128)} %fusion.29, f32[16,256,256]{2,1,0:T(8,128)} %fusion.32, f32[16,256,256]{2,1,0:T(8,128)} %fusion.33, f32[256,16,256]{0,2,1:T(8,128)S(1)} %fusion.41, f32[16,256,256]{2,1,0:T(8,128)} %fusion.34, f32[16,256,256]{2,1,0:T(8,128)} %fusion.35, ...), kind=kOutput, calls=%fused_computation.17 | convolution fusion | flops 548405248 | bytes 37880840 | tf_op jit(solution)/shard_map/shwc,co->shwo/dot_general | solution.py:34
  110.0 1.5 fusion.58
  111.5 4.3 %collective-permute-start.5 = (bf16[1,8,256,256]{3,2,1,0:T(8,128)(2,1)}, bf16[1,8,256,256]{3,2,1,0:T(8,128)(2,1)S(1)}, u32[]{:S(2)}, u32[]{:S(2)}) collective-permute-start(bf16[1,8,256,256]{3,2,1,0:T(8,128)(2,1)} %get-tuple-element.5), channel_id=1, source_target_pairs={{0,1},{1,2},{2,3},{4,5},{5,6},{6,7},{8,9},{9,10},{10,11},{12,13},{... | collective-permute-start | bytes 3145736 | tf_op jit(solution)/shard_map/ppermute | solution.py:14
  115.7 2.1 %collective-permute-start.6 = (bf16[1,8,256,256]{3,2,1,0:T(8,128)(2,1)}, bf16[1,8,256,256]{3,2,1,0:T(8,128)(2,1)}, u32[]{:S(2)}, u32[]{:S(2)}) collective-permute-start(bf16[1,8,256,256]{3,2,1,0:T(8,128)(2,1)} %get-tuple-element.6), channel_id=1, source_target_pairs={{1,0},{2,1},{3,2},{5,4},{6,5},{7,6},{9,8},{10,9},{11,10},{13,12},{... | collective-permute-start | bytes 3145736 | tf_op jit(solution)/shard_map/ppermute | solution.py:17
  117.9 3.7 %fusion.44 = f32[16,256,256]{2,1,0:T(8,128)} fusion(bf16[16,256,256]{2,1,0:T(8,128)(2,1)S(1)} %fusion.12, bf16[3,3,256,256]{2,3,1,0:T(8,128)(2,1)} %all-gather.2.cloned.1.call-done), kind=kOutput, calls=%fused_computation.69 | convolution fusion | flops 536870912 | bytes 6422528 | tf_op jit(solution)/shard_map/shwc,co->shwo/dot_general | solution.py:34
  121.6 6.2 %collective-permute-done.5 = bf16[1,8,256,256]{3,2,1,0:T(8,128)(2,1)S(1)} collective-permute-done((bf16[1,8,256,256]{3,2,1,0:T(8,128)(2,1)}, bf16[1,8,256,256]{3,2,1,0:T(8,128)(2,1)S(1)}, u32[]{:S(2)}, u32[]{:S(2)}) %collective-permute-start.5) | collective-permute-done | bytes 1048608 | tf_op jit(solution)/shard_map/ppermute | solution.py:14
  127.8 2.7 %fusion.23 = f32[16,256,256]{2,1,0:T(8,128)} fusion(bf16[1,16,256,256]{3,2,1,0:T(8,128)(2,1)S(1)} %bitcast.177, bf16[1,8,256,256]{3,2,1,0:T(8,128)(2,1)S(1)} %collective-permute-done.5, bf16[3,3,256,256]{2,3,1,0:T(8,128)(2,1)S(1)} %copy-done.3), kind=kOutput, calls=%fused_computation.35 | convolution fusion | flops 537919488 | bytes 7471104 | tf_op jit(solution)/shard_map/shwc,co->shwo/dot_general | solution.py:34
  130.5 1.7 collective-permute-done.6
  132.2 4.0 %fusion.15 = f32[16,256,256]{2,1,0:T(8,128)} fusion(bf16[1,8,256,256]{3,2,1,0:T(8,128)(2,1)} %collective-permute-done.6, bf16[1,16,256,256]{3,2,1,0:T(8,128)(2,1)S(1)} %bitcast.178, bf16[3,3,256,256]{2,3,1,0:T(8,128)(2,1)S(1)} %copy-done.3), kind=kOutput, calls=%fused_computation.23 | convolution fusion | flops 537919488 | bytes 7471104 | tf_op jit(solution)/shard_map/shwc,co->shwo/dot_general | solution.py:34
  136.1 1.9 %select_maximum_fusion = bf16[1,32,272,256]{3,2,1,0:T(8,128)(2,1)S(1)} fusion(bf16[1,8,256,256]{3,2,1,0:T(8,128)(2,1)} %collective-permute-done.6, bf16[1,16,256,256]{3,2,1,0:T(8,128)(2,1)S(1)} %bitcast.179, bf16[1,8,256,256]{3,2,1,0:T(8,128)(2,1)S(1)} %collective-permute-done.5), kind=kLoop, calls=%fused_computation.3 | loop fusion | flops 26738688 | bytes 8650752 | tf_op jit(solution)/shard_map/concatenate | solution.py:18
  138.1 2.7 %fusion.18 = f32[16,256,256]{2,1,0:T(8,128)} fusion(bf16[1,32,272,256]{3,2,1,0:T(8,128)(2,1)S(1)} %select_maximum_fusion, bf16[3,3,256,256]{2,3,1,0:T(8,128)(2,1)S(1)} %copy-done.3), kind=kOutput, calls=%fused_computation.26 | convolution fusion | flops 536870912 | bytes 6422528 | tf_op jit(solution)/shard_map/shwc,co->shwo/dot_general | solution.py:34
  140.8 2.7 %fusion.19 = f32[16,256,256]{2,1,0:T(8,128)} fusion(bf16[1,32,272,256]{3,2,1,0:T(8,128)(2,1)S(1)} %select_maximum_fusion, bf16[3,3,256,256]{2,3,1,0:T(8,128)(2,1)S(1)} %copy-done.3), kind=kOutput, calls=%fused_computation.28 | convolution fusion | flops 536870912 | bytes 6422528 | tf_op jit(solution)/shard_map/shwc,co->shwo/dot_general | solution.py:34
  143.5 2.7 %fusion.20 = f32[16,256,256]{2,1,0:T(8,128)} fusion(bf16[1,32,272,256]{3,2,1,0:T(8,128)(2,1)S(1)} %select_maximum_fusion, bf16[3,3,256,256]{2,3,1,0:T(8,128)(2,1)S(1)} %copy-done.3), kind=kOutput, calls=%fused_computation.30 | convolution fusion | flops 536870912 | bytes 6422528 | tf_op jit(solution)/shard_map/shwc,co->shwo/dot_general | solution.py:34
  146.2 2.7 %fusion.21 = f32[16,256,256]{2,1,0:T(8,128)} fusion(bf16[1,32,272,256]{3,2,1,0:T(8,128)(2,1)S(1)} %select_maximum_fusion, bf16[3,3,256,256]{2,3,1,0:T(8,128)(2,1)S(1)} %copy-done.3), kind=kOutput, calls=%fused_computation.32 | convolution fusion | flops 536870912 | bytes 6422528 | tf_op jit(solution)/shard_map/shwc,co->shwo/dot_general | solution.py:34
  148.9 2.8 %fusion.26 = f32[16,256,256]{2,1,0:T(8,128)} fusion(bf16[1,32,272,256]{3,2,1,0:T(8,128)(2,1)S(1)} %select_maximum_fusion, bf16[3,3,256,256]{2,3,1,0:T(8,128)(2,1)S(1)} %copy-done.3), kind=kOutput, calls=%fused_computation.38 | convolution fusion | flops 536870912 | bytes 6422528 | tf_op jit(solution)/shard_map/shwc,co->shwo/dot_general | solution.py:34
  152.3 12.1 %fusion.43 = bf16[1,16,256,256]{3,2,1,0:T(8,128)(2,1)} fusion(f32[256]{0:T(256)S(1)} %copy-done.6, bf16[1,32,272,256]{3,2,1,0:T(8,128)(2,1)S(1)} %select_maximum_fusion, f32[16,256,256]{2,1,0:T(8,128)} %fusion.15, f32[16,256,256]{2,1,0:T(8,128)} %fusion.18, f32[16,256,256]{2,1,0:T(8,128)} %fusion.19, f32[16,256,256]{2,1,0:T(8,128)} %fusion.44, ...), kind=kOutput, calls=%fused_computation.61 | convolution fusion | flops 548405248 | bytes 37880832 | tf_op jit(solution)/shard_map/shwc,co->shwo/dot_general | solution.py:34
  (27 shorter events, 6.0 us)
Async XLA Ops:
  6.5 19.9 %copy-start.4 = (bf16[3,3,256,32]{2,3,1,0:T(8,128)(2,1)S(1)}, bf16[3,3,256,32]{2,3,1,0:T(8,128)(2,1)}, u32[]{:S(2)}) copy-start(bf16[3,3,256,32]{2,3,1,0:T(8,128)(2,1)} %param.6) | copy-start | bytes 442372
  6.5 111.3 %all-gather.2.cloned.1.call-start = ((), (), s32[]{:S(2)}) async-start(), calls=%async_computation | async-start | bytes 1327104 | tf_op jit(solution)/shard_map/all_gather | solution.py:58
  6.5 7.9 %collective-permute-start.2 = (bf16[3,3,256,32]{2,3,1,0:T(8,128)(2,1)}, bf16[3,3,256,32]{2,3,1,0:T(8,128)(2,1)S(1)}, u32[]{:S(2)}, u32[]{:S(2)}) collective-permute-start(bf16[3,3,256,32]{2,3,1,0:T(8,128)(2,1)} %param.6), channel_id=1, source_target_pairs={{0,28},{4,0},{8,4},{12,8},{16,12},{20,16},{24,20},{28,24},{1,29},{... | collective-permute-start | bytes 442376 | tf_op jit(solution)/shard_map/ppermute | solution.py:49
  15.4 11.7 %collective-permute-start.3 = (bf16[3,3,256,64]{2,3,1,0:T(8,128)(2,1)S(1)}, bf16[3,3,256,64]{2,3,1,0:T(8,128)(2,1)S(1)}, u32[]{:S(2)}, u32[]{:S(2)}) collective-permute-start(bf16[3,3,256,64]{2,3,1,0:T(8,128)(2,1)S(1)} %pad_maximum_fusion.5), channel_id=1, source_target_pairs={{0,24},{4,28},{8,0},{12,4},{16,8},{20,12},{24,16},{28,20},{1,25},{... | collective-permute-start | bytes 884744 | tf_op jit(solution)/shard_map/ppermute | solution.py:49
  19.7 51.4 %collective-permute-start = (bf16[1,8,256,256]{3,2,1,0:T(8,128)(2,1)}, bf16[1,8,256,256]{3,2,1,0:T(8,128)(2,1)}, u32[]{:S(2)}, u32[]{:S(2)}) collective-permute-start(bf16[1,8,256,256]{3,2,1,0:T(8,128)(2,1)} %get-tuple-element.7), channel_id=1, source_target_pairs={{0,1},{1,2},{2,3},{4,5},{5,6},{6,7},{8,9},{9,10},{10,11},{12,13},{... | collective-permute-start | bytes 3145736 | tf_op jit(solution)/shard_map/ppermute | solution.py:14
  24.5 46.6 %collective-permute-start.1 = (bf16[1,8,256,256]{3,2,1,0:T(8,128)(2,1)}, bf16[1,8,256,256]{3,2,1,0:T(8,128)(2,1)}, u32[]{:S(2)}, u32[]{:S(2)}) collective-permute-start(bf16[1,8,256,256]{3,2,1,0:T(8,128)(2,1)} %get-tuple-element.8), channel_id=1, source_target_pairs={{1,0},{2,1},{3,2},{5,4},{6,5},{7,6},{9,8},{10,9},{11,10},{13,12},{... | collective-permute-start | bytes 3145736 | tf_op jit(solution)/shard_map/ppermute | solution.py:17
  27.4 0.8 copy-start.2
  29.6 39.8 %copy-start = (bf16[1,16,256,256]{3,2,1,0:T(8,128)(2,1)S(1)}, bf16[1,16,256,256]{3,2,1,0:T(8,128)(2,1)}, u32[]{:S(2)}) copy-start(bf16[1,16,256,256]{3,2,1,0:T(8,128)(2,1)} %param.5) | copy-start | bytes 6291460
  29.6 33.0 %collective-permute-start.4 = (bf16[3,3,256,128]{3,2,1,0:T(8,128)(2,1)}, bf16[3,3,256,128]{3,2,1,0:T(8,128)(2,1)}, u32[]{:S(2)}, u32[]{:S(2)}) collective-permute-start(bf16[3,3,256,128]{3,2,1,0:T(8,128)(2,1)} %pad_maximum_fusion.4), channel_id=1, source_target_pairs={{0,16},{4,20},{8,24},{12,28},{16,0},{20,4},{24,8},{28,12},{1,17},{... | collective-permute-start | bytes 1769480 | tf_op jit(solution)/shard_map/ppermute | solution.py:49
  95.4 4.0 %copy-start.5 = (f32[256]{0:T(256)S(1)}, f32[256]{0:T(256)}, u32[]{:S(2)}) copy-start(f32[256]{0:T(256)} %param.7) | copy-start | bytes 3076
  111.5 16.3 %collective-permute-start.5 = (bf16[1,8,256,256]{3,2,1,0:T(8,128)(2,1)}, bf16[1,8,256,256]{3,2,1,0:T(8,128)(2,1)S(1)}, u32[]{:S(2)}, u32[]{:S(2)}) collective-permute-start(bf16[1,8,256,256]{3,2,1,0:T(8,128)(2,1)} %get-tuple-element.5), channel_id=1, source_target_pairs={{0,1},{1,2},{2,3},{4,5},{5,6},{6,7},{8,9},{9,10},{10,11},{12,13},{... | collective-permute-start | bytes 3145736 | tf_op jit(solution)/shard_map/ppermute | solution.py:14
  115.7 16.4 %collective-permute-start.6 = (bf16[1,8,256,256]{3,2,1,0:T(8,128)(2,1)}, bf16[1,8,256,256]{3,2,1,0:T(8,128)(2,1)}, u32[]{:S(2)}, u32[]{:S(2)}) collective-permute-start(bf16[1,8,256,256]{3,2,1,0:T(8,128)(2,1)} %get-tuple-element.6), channel_id=1, source_target_pairs={{1,0},{2,1},{3,2},{5,4},{6,5},{7,6},{9,8},{10,9},{11,10},{13,12},{... | collective-permute-start | bytes 3145736 | tf_op jit(solution)/shard_map/ppermute | solution.py:17
  117.9 9.9 %copy-start.3 = (bf16[3,3,256,256]{2,3,1,0:T(8,128)(2,1)S(1)}, bf16[3,3,256,256]{2,3,1,0:T(8,128)(2,1)}, u32[]{:S(2)}) copy-start(bf16[3,3,256,256]{2,3,1,0:T(8,128)(2,1)} %all-gather.2.cloned.1.call-done) | copy-start | bytes 3538948
  148.9 3.4 %copy-start.1 = (f32[16,256,256]{2,1,0:T(8,128)S(1)}, f32[16,256,256]{2,1,0:T(8,128)}, u32[]{:S(2)}) copy-start(f32[16,256,256]{2,1,0:T(8,128)} %fusion.23) | copy-start | bytes 12582916
  148.9 3.4 %copy-start.6 = (f32[256]{0:T(256)S(1)}, f32[256]{0:T(256)}, u32[]{:S(2)}) copy-start(f32[256]{0:T(256)} %param.9) | copy-start | bytes 3076
Sparse Core Ops, SparseCore 0:
  29.8 52.1 all-gather.1
